TPU v7x, 256 devices: a whole 4x4x8 slice. The times are simulated.
256 devices in a mesh: row: 8 (over z_hi, y), col: 16 (over x, z_lo), rep: 2 (over core).
Axes of the slice: x: 4, y: 4, z: 8 (z_hi: 2, z_lo: 4; z = z_hi * 4 + z_lo), core: 2. Of those that a mesh axis runs over, the one named last changes fastest.
Arguments:
- ancestor_inverse: float32 [16384, 16384], P('row', 'col'), may hold values from -6 to 6
- tile_structure: int32 [128, 128], P('row', 'col'), may hold values from 0 to 1, as said below
- factor: float32 [16384, 512], P(('row', 'col')), may hold values from -0.046875 to 0.046875
- factor_normalizer: float32 [512, 512], replicated, may hold values from -1 to 1, as said below
- pivot_inverse: float32 [512, 512], P(None, 'rep'), may hold values from -6 to 6, as said below
Outputs:
- ancestor_columns: float32 [16384, 512], P(('row', 'col'), 'rep')
- diag_block: float32 [512, 512], P(None, 'rep')
Inputs may be any that keep to these rules, and one draw needn't show every extreme that they name: `tile_structure`: symmetric, with ones on the diagonal. `factor_normalizer`: lower triangular with ones on its diagonal. `pivot_inverse`: symmetric.
All inputs are finite; a program needn't handle non-finite values.
Results may differ from a plain program's by a relative error of at most 0.000078.
Values sent between devices are 32-bit elements; how exact they have to be, the bound alone decides.
A program may use at most 64 MiB of HBM per device.

v0:
```python
import jax
import jax.numpy as jnp
from jax import lax
from jax.sharding import PartitionSpec as P


def spread(block, axis, owner):
    block = jnp.where(lax.axis_index(axis) == owner, block, jnp.zeros_like(block))
    return lax.psum(block, axis)


def partner(block, axis, distance):
    count = lax.axis_size(axis)
    route = []
    for low in range(count):
        high = low | 1 << distance
        if high != low and high < count:
            route += [(low, high), (high, low)]
    return lax.ppermute(block, axis, route)


def contract_rows(left, right):
    return lax.dot_general(
        left,
        right,
        (((0,), (0,)), ((), ())),
        precision=lax.Precision.HIGHEST,
        preferred_element_type=jnp.float32,
    )


def body(ancestor_inverse, tile_structure, factor, factor_normalizer, pivot_inverse):
    tile_rows = factor.shape[0]
    half_width = pivot_inverse.shape[1]
    copy_index = lax.axis_index("rep")
    column_index = lax.axis_index("col")
    row_count = lax.axis_size("row")
    column_count = lax.axis_size("col")
    column_ratio = column_count // row_count
    block_rows = tile_rows * row_count
    normed = jnp.dot(
        factor,
        factor_normalizer,
        precision=lax.Precision.HIGHEST,
        preferred_element_type=jnp.float32,
    )
    own_columns = lax.dynamic_slice_in_dim(normed, copy_index * half_width, half_width, 1)
    gathered = lax.all_gather(own_columns, "col", axis=0, tiled=True)
    shared = spread(gathered, "row", column_index // column_ratio)
    column_block = lax.dynamic_slice_in_dim(
        shared, column_index % column_ratio * block_rows, block_rows, 0
    )
    tile_marks = tile_structure.astype(jnp.float32)
    across = ancestor_inverse.shape[1] // tile_rows
    masked = (
        ancestor_inverse.reshape(
            tile_rows * lax.axis_size("col") // tile_rows, tile_rows, across, tile_rows
        )
        * tile_marks[:, None, :, None]
    ).reshape(tile_rows * lax.axis_size("col"), across * tile_rows)
    ancestor_columns = lax.psum_scatter(
        -jnp.dot(
            masked,
            column_block,
            precision=lax.Precision.HIGHEST,
            preferred_element_type=jnp.float32,
        ),
        "col",
        scatter_dimension=0,
        tiled=True,
    )
    coupling_term = contract_rows(normed, ancestor_columns)
    coupling = lax.psum(coupling_term, ("row", "col"))
    outgoing_rows = lax.dynamic_slice_in_dim(coupling, (1 - copy_index) * half_width, half_width, 0)
    incoming = partner(outgoing_rows, "rep", 0)
    own_block = lax.dynamic_slice_in_dim(coupling, copy_index * half_width, half_width, 0)
    mirrored = jnp.where(
        copy_index == 0,
        jnp.concatenate([own_block, incoming], 1),
        jnp.concatenate([incoming, own_block], 1),
    )
    diag_block = pivot_inverse - 0.5 * (coupling + mirrored.T)
    return (ancestor_columns, diag_block)


def solution(mesh):
    return jax.shard_map(
        body,
        mesh=mesh,
        in_specs=(P("row", "col"), P("row", "col"), P(("row", "col"), None), P(), P(None, "rep")),
        out_specs=(P(("row", "col"), "rep"), P(None, "rep")),
        check_vma=False,
    )
```

profile of v0, /device:TPU:1, one launch (start us, length us, event | category | flops | bytes accessed | tf_op | source)
XLA Modules:
  0.0 569.2 jit_solution(9534586514955601280)
XLA Ops:
  7.2 0.0 copy-start
  7.2 0.0 all-gather.2.cloned.1.call-start
  7.2 1.2 copy-done
  8.4 1.7 fusion.9
  10.1 0.7 constant_dynamic-slice_fusion.2
  10.7 0.0 all-gather.2.cloned.1.call-update
  10.8 0.0 all-reduce.3.cloned.1.call-start
  10.8 82.3 %all-gather.2.cloned.1.call-done = f32[2048,256]{1,0:T(8,128)} async-done(((f32[128,256]{1,0:T(8,128)}), f32[2048,256]{1,0:T(8,128)}) %all-gather.2.cloned.1.call-update) | async-done | bytes 2097168 | tf_op jit(solution)/shard_map/all_gather | solution.py:48
  93.1 3.1 broadcast_select_fusion
  96.2 0.0 copy-start.4
  96.2 0.0 all-reduce.3.cloned.1.call-update
  96.2 0.0 reduce-scatter.2.cloned.1.call-start
  96.3 0.6 copy-done.4
  96.9 0.1 copy.7
  96.9 138.5 %all-reduce.3.cloned.1.call-done = f32[2048,256]{1,0:T(8,128)} async-done(((f32[2048,256]{1,0:T(8,128)}), f32[2048,256]{1,0:T(8,128)}) %all-reduce.3.cloned.1.call-update) | async-done | bytes 2097168 | tf_op jit(solution)/shard_map/psum | solution.py:9
  235.4 0.0 copy-start.2
  235.4 0.6 mul.27
  236.0 1.0 copy-done.2
  237.0 10.5 %fusion.2 = f32[2048,256]{1,0:T(8,128)} fusion(f32[2048,1024]{1,0:T(8,128)} %param.5, f32[256,8,8,128]{3,2,1,0:T(8,128)S(1)} %bitcast.19, f32[2048,256]{1,0:T(8,128)S(1)} %copy-done.2, s32[]{:T(128)S(6)} %select_n.42), kind=kOutput, calls=%fused_computation.3 | convolution fusion | flops 6445072384 | bytes 19922948 | tf_op jit(solution)/shard_map/dot_general | solution.py:62
  247.5 0.0 reduce-scatter.2.cloned.1.call-update
  247.6 0.0 copy-start.3
  247.6 0.0 all-reduce.5.cloned.1.call-start
  247.6 81.7 %reduce-scatter.2.cloned.1.call-done = f32[128,256]{1,0:T(8,128)} async-done(((f32[2048,256]{1,0:T(8,128)}), f32[128,256]{1,0:T(8,128)}) %reduce-scatter.2.cloned.1.call-update) | async-done | bytes 131088 | tf_op jit(solution)/shard_map/reduce_scatter | solution.py:61
  329.3 2.3 fusion.10
  331.6 0.0 all-reduce.5.cloned.1.call-update
  331.7 222.4 %all-reduce.5.cloned.1.call-done = f32[512,256]{1,0:T(8,128)} async-done(((f32[512,256]{1,0:T(8,128)}), f32[512,256]{1,0:T(8,128)}) %all-reduce.5.cloned.1.call-update) | async-done | bytes 524304 | tf_op jit(solution)/shard_map/psum | solution.py:73
  554.0 0.0 copy-start.1
  554.0 1.1 constant_dynamic-slice_fusion.1
  555.1 0.1 copy.11
  555.3 5.3 collective-permute-start
  560.6 0.1 copy.10
  560.7 1.0 collective-permute-done
  561.7 0.0 copy-done.3
  561.7 0.0 copy-done.1
  561.7 0.9 fusion.7
  (1 shorter events, 0.0 us)
Async XLA Ops:
  7.2 1.2 copy-start
  7.2 85.9 %all-gather.2.cloned.1.call-start = ((), (), s32[]{:S(2)}) async-start(), calls=%async_computation.1 | async-start | bytes 2228224 | tf_op jit(solution)/shard_map/all_gather | solution.py:48
  10.8 224.7 %all-reduce.3.cloned.1.call-start = ((), (), s32[]{:S(2)}) async-start(), calls=%async_computation.2 | async-start | bytes 4194304 | tf_op jit(solution)/shard_map/psum | solution.py:9
  96.2 0.7 copy-start.4
  96.2 233.1 %reduce-scatter.2.cloned.1.call-start = ((), (), s32[]{:S(2)}) async-start(), calls=%async_computation.3 | async-start | bytes 2228224 | tf_op jit(solution)/shard_map/reduce_scatter | solution.py:61
  235.4 1.6 copy-start.2
  247.6 314.2 %copy-start.3 = (f32[512,256]{1,0:T(8,128)S(1)}, f32[512,256]{1,0:T(8,128)}, u32[]{:S(2)}) copy-start(f32[512,256]{1,0:T(8,128)} %param.9) | copy-start | bytes 1572868
  247.6 306.4 %all-reduce.5.cloned.1.call-start = ((), (), s32[]{:S(2)}) async-start(), calls=%async_computation.4 | async-start | bytes 1048576 | tf_op jit(solution)/shard_map/psum | solution.py:73
  554.0 7.7 %copy-start.1 = (f32[512,256]{1,0:T(8,128)S(1)}, f32[512,256]{1,0:T(8,128)}, u32[]{:S(2)}) copy-start(f32[512,256]{1,0:T(8,128)} %all-reduce.5.cloned.1.call-done) | copy-start | bytes 1572868
  555.3 6.4 %collective-permute-start = (f32[256,256]{0,1:T(8,128)S(1)}, f32[256,256]{0,1:T(8,128)S(1)}, u32[]{:S(2)}, u32[]{:S(2)}) collective-permute-start(f32[256,256]{0,1:T(8,128)S(1)} %copy.11), channel_id=1, source_target_pairs={{0,1},{1,0},{2,3},{3,2},{4,5},{5,4},{6,7},{7,6},{8,9},{9,8},{10,11... | collective-permute-start | bytes 786440 | tf_op jit(solution)/shard_map/ppermute | solution.py:19
Sparse Core Ops, SparseCore 0:
  10.9 82.1 all-gather.1
  96.3 139.0 all-reduce.2
  247.7 81.5 reduce-scatter.1
  335.2 218.8 all-reduce.4
where the time goes:
time: 569 us
  waiting for transfers between devices  526 us (92%)
  matrix products  14.5 us (3%)
  between operations  13.9 us (2%)
    psum x1, waiting for transfers between devices, body(): coupling = lax.psum(coupling_term, ('row', 'col'))  222 us
    psum x1, waiting for transfers between devices, spread(): return lax.psum(block, axis)  138 us
    all_gather x1, waiting for transfers between devices, body(): gathered = lax.all_gather(own_columns, 'col', axis=0, tiled=True)  82.3 us
    reduce_scatter x1, waiting for transfers between devices, body(): lax.psum_scatter(-jnp.dot(masked, column_block, precision=lax.Precision.H...  81.7 us
  transfers between devices with their start and end apart: 5, of which 5 were waited for; matrix products, arithmetic and copies ran while one was open for 0% of the time, Pallas kernels for 0%

commit v1 on v0

--- a/solution.py
+++ b/solution.py
@@ -6,7 +6,7 @@
 
 def spread(block, axis, owner):
     block = jnp.where(lax.axis_index(axis) == owner, block, jnp.zeros_like(block))
-    return lax.psum(block, axis)
+    return jnp.sum(lax.all_gather(block, axis), axis=0)
 
 
 def partner(block, axis, distance):

time: 569 us -> 745 us (1.31)
  waiting for transfers between devices: 526 us -> 696 us
    all_gather x0 -> x1, waiting for transfers between devices: none -> 314 us  [spread(): return jnp.sum(lax.all_gather(block, axis), axis=0)]
    psum x1 -> x0, waiting for transfers between devices: 138 us -> none  [spread(): return lax.psum(block, axis)]
where the time goes in v1:
time: 745 us
  waiting for transfers between devices  696 us (93%)
  matrix products  14.5 us (2%)
  between operations  13.9 us (2%)
  other arithmetic  11.1 us (1%)
    all_gather x1, waiting for transfers between devices, spread(): return jnp.sum(lax.all_gather(block, axis), axis=0)  314 us
    psum x1, waiting for transfers between devices, body(): coupling = lax.psum(coupling_term, ('row', 'col'))  223 us
    all_gather x1, waiting for transfers between devices, body(): gathered = lax.all_gather(own_columns, 'col', axis=0, tiled=True)  82.3 us
    reduce_scatter x1, waiting for transfers between devices, body(): lax.psum_scatter(-jnp.dot(masked, column_block, precision=lax.Precision.H...  76.1 us
  transfers between devices with their start and end apart: 5, of which 5 were waited for; matrix products, arithmetic and copies ran while one was open for 0% of the time, Pallas kernels for 0%

profile of v1, /device:TPU:1, one launch (start us, length us, event | category | flops | bytes accessed | tf_op | source)
XLA Modules:
  0.0 745.1 jit_solution(11564645330830692076)
XLA Ops:
  7.2 0.0 copy-start
  7.2 0.0 all-gather.4.cloned.1.call-start
  7.2 1.2 copy-done
  8.4 1.7 fusion.9
  10.1 0.7 constant_dynamic-slice_fusion.2
  10.7 0.0 all-gather.4.cloned.1.call-update
  10.8 0.0 all-gather.6.cloned.1.call-start
  10.8 82.3 %all-gather.4.cloned.1.call-done = f32[2048,256]{1,0:T(8,128)} async-done(((f32[128,256]{1,0:T(8,128)}), f32[2048,256]{1,0:T(8,128)}) %all-gather.4.cloned.1.call-update) | async-done | bytes 2097168 | tf_op jit(solution)/shard_map/all_gather | solution.py:48
  93.1 3.1 broadcast_select_fusion
  96.2 0.0 copy-start.3
  96.2 0.0 all-gather.6.cloned.1.call-update
  96.2 0.0 reduce-scatter.2.cloned.1.call-start
  96.3 0.6 copy-done.3
  96.9 0.1 copy.7
  96.9 313.6 %all-gather.6.cloned.1.call-done = f32[16384,256]{1,0:T(8,128)} async-done(((f32[2048,256]{1,0:T(8,128)}), f32[16384,256]{1,0:T(8,128)}) %all-gather.6.cloned.1.call-update) | async-done | bytes 16777232 | tf_op jit(solution)/shard_map/all_gather | solution.py:9
  410.5 7.1 reduce_sum.9
  417.7 0.6 mul.27
  418.3 10.5 %fusion.2 = f32[2048,256]{1,0:T(8,128)} fusion(f32[2048,1024]{1,0:T(8,128)} %param.5, f32[256,8,8,128]{3,2,1,0:T(8,128)S(1)} %bitcast.20, f32[2048,256]{1,0:T(8,128)S(1)} %reduce_sum.9, s32[]{:T(128)S(6)} %select_n.42), kind=kOutput, calls=%fused_computation.3 | convolution fusion | flops 6445072384 | bytes 19922948 | tf_op jit(solution)/shard_map/dot_general | solution.py:62
  428.8 0.0 reduce-scatter.2.cloned.1.call-update
  428.8 0.0 copy-start.2
  428.8 0.0 all-reduce.2.cloned.1.call-start
  428.9 76.1 %reduce-scatter.2.cloned.1.call-done = f32[128,256]{1,0:T(8,128)} async-done(((f32[2048,256]{1,0:T(8,128)}), f32[128,256]{1,0:T(8,128)}) %reduce-scatter.2.cloned.1.call-update) | async-done | bytes 131088 | tf_op jit(solution)/shard_map/reduce_scatter | solution.py:61
  504.9 2.3 fusion.10
  507.3 0.0 all-reduce.2.cloned.1.call-update
  507.3 222.6 %all-reduce.2.cloned.1.call-done = f32[512,256]{1,0:T(8,128)} async-done(((f32[512,256]{1,0:T(8,128)}), f32[512,256]{1,0:T(8,128)}) %all-reduce.2.cloned.1.call-update) | async-done | bytes 524304 | tf_op jit(solution)/shard_map/psum | solution.py:73
  729.9 0.0 copy-start.1
  729.9 1.1 constant_dynamic-slice_fusion.1
  731.1 0.1 copy.11
  731.2 5.3 collective-permute-start
  736.5 0.1 copy.10
  736.6 1.0 collective-permute-done
  737.6 0.0 copy-done.2
  737.6 0.0 copy-done.1
  737.6 0.9 fusion.7
  (1 shorter events, 0.0 us)
Async XLA Ops:
  7.2 1.2 copy-start
  7.2 85.9 %all-gather.4.cloned.1.call-start = ((), (), s32[]{:S(2)}) async-start(), calls=%async_computation.1 | async-start | bytes 2228224 | tf_op jit(solution)/shard_map/all_gather | solution.py:48
  10.8 399.8 %all-gather.6.cloned.1.call-start = ((), (), s32[]{:S(2)}) async-start(), calls=%async_computation.4 | async-start | bytes 18874368 | tf_op jit(solution)/shard_map/all_gather | solution.py:9
  96.2 0.7 copy-start.3
  96.2 408.7 %reduce-scatter.2.cloned.1.call-start = ((), (), s32[]{:S(2)}) async-start(), calls=%async_computation.2 | async-start | bytes 2228224 | tf_op jit(solution)/shard_map/reduce_scatter | solution.py:61
  428.8 308.8 %copy-start.2 = (f32[512,256]{1,0:T(8,128)S(1)}, f32[512,256]{1,0:T(8,128)}, u32[]{:S(2)}) copy-start(f32[512,256]{1,0:T(8,128)} %param.9) | copy-start | bytes 1572868
  428.8 301.1 %all-reduce.2.cloned.1.call-start = ((), (), s32[]{:S(2)}) async-start(), calls=%async_computation.3 | async-start | bytes 1048576 | tf_op jit(solution)/shard_map/psum | solution.py:73
  729.9 7.7 %copy-start.1 = (f32[512,256]{1,0:T(8,128)S(1)}, f32[512,256]{1,0:T(8,128)}, u32[]{:S(2)}) copy-start(f32[512,256]{1,0:T(8,128)} %all-reduce.2.cloned.1.call-done) | copy-start | bytes 1572868
  731.2 6.4 collective-permute-start
Sparse Core Ops, SparseCore 0:
  10.9 82.1 all-gather.3
  96.3 314.1 all-gather.5
  428.9 75.9 reduce-scatter.1
  510.8 219.0 all-reduce.1

commit v2 on v0

--- a/solution.py
+++ b/solution.py
@@ -45,7 +45,9 @@
         preferred_element_type=jnp.float32,
     )
     own_columns = lax.dynamic_slice_in_dim(normed, copy_index * half_width, half_width, 1)
-    gathered = lax.all_gather(own_columns, "col", axis=0, tiled=True)
+    gathered = jnp.concatenate(
+        lax.all_to_all(jnp.stack([own_columns] * lax.axis_size("col")), "col", 0, 0), axis=0
+    )
     shared = spread(gathered, "row", column_index // column_ratio)
     column_block = lax.dynamic_slice_in_dim(
         shared, column_index % column_ratio * block_rows, block_rows, 0

time: 569 us -> 538 us (0.946)
  waiting for transfers between devices: 526 us -> 486 us
  starting transfers between devices: 5.44 us -> 14.4 us
    all_gather x1 -> x0, waiting for transfers between devices: 82.3 us -> none  [body(): gathered = lax.all_gather(own_columns, 'col', axis=0, tiled=True)]
    all_to_all x0 -> x1, waiting for transfers between devices: none -> 49.7 us  [body(): lax.all_to_all(jnp.stack([own_columns] * lax.axis_size('col')), 'col', 0, 0)]
    all_to_all x0 -> x1, starting transfers between devices: none -> 9.02 us  [body(): lax.all_to_all(jnp.stack([own_columns] * lax.axis_size('col')), 'col', 0, 0)]
    psum x1, waiting for transfers between devices: 138 us -> 130 us  [spread(): return lax.psum(block, axis)]
where the time goes in v2:
time: 538 us; the launch traced here: 537 us
  waiting for transfers between devices  486 us (90%)
  matrix products  14.5 us (3%)
  starting transfers between devices  14.4 us (3%)
  between operations  13.9 us (3%)
  local copies, waits for them, and re-layouts  6.42 us (1%)
    psum x1, waiting for transfers between devices, body(): coupling = lax.psum(coupling_term, ('row', 'col'))  223 us
    psum x1, waiting for transfers between devices, spread(): return lax.psum(block, axis)  130 us
    reduce_scatter x1, waiting for transfers between devices, body(): lax.psum_scatter(-jnp.dot(masked, column_block, precision=lax.Precision.H...  81.7 us
    all_to_all x1, waiting for transfers between devices, body(): lax.all_to_all(jnp.stack([own_columns] * lax.axis_size('col')), 'col', 0, 0)  49.7 us
  transfers between devices with their start and end apart: 5, of which 5 were waited for; matrix products, arithmetic and copies ran while one was open for 0% of the time, Pallas kernels for 0%

profile of v2, /device:TPU:1, one launch (start us, length us, event | category | flops | bytes accessed | tf_op | source)
XLA Modules:
  0.0 537.3 jit_solution(2869457468529821402)
XLA Ops:
  7.2 0.0 copy-start
  7.2 1.2 copy-done
  8.4 1.7 fusion.9
  10.1 1.5 stack.2
  11.6 9.0 %all-to-all-start = ((f32[16,128,256]{2,1,0:T(8,128)}), f32[16,128,256]{2,1,0:T(8,128)S(1)}, u32[]{:S(2)}, u32[]{:S(2)}) async-start(f32[16,128,256]{2,1,0:T(8,128)} %stack.2), calls=%async_computation | async-start | bytes 4194304 | tf_op jit(solution)/shard_map/all_to_all | solution.py:49
  20.7 0.0 all-reduce.3.cloned.1.call-start
  20.7 49.7 %all-to-all-done = f32[16,128,256]{2,1,0:T(8,128)S(1)} async-done(((f32[16,128,256]{2,1,0:T(8,128)}), f32[16,128,256]{2,1,0:T(8,128)S(1)}, u32[]{:S(2)}, u32[]{:S(2)}) %all-to-all-start) | async-done | bytes 2097184 | tf_op jit(solution)/shard_map/all_to_all | solution.py:49
  70.4 1.6 broadcast_select_fusion
  72.0 0.0 copy-start.4
  72.0 0.0 all-reduce.3.cloned.1.call-update
  72.0 0.0 reduce-scatter.2.cloned.1.call-start
  72.1 0.6 copy-done.4
  72.7 0.1 copy.7
  72.8 130.3 %all-reduce.3.cloned.1.call-done = f32[2048,256]{1,0:T(8,128)} async-done(((f32[2048,256]{1,0:T(8,128)}), f32[2048,256]{1,0:T(8,128)}) %all-reduce.3.cloned.1.call-update) | async-done | bytes 2097168 | tf_op jit(solution)/shard_map/psum | solution.py:9
  203.0 0.0 copy-start.2
  203.0 0.6 mul.27
  203.6 1.0 copy-done.2
  204.6 10.5 %fusion.2 = f32[2048,256]{1,0:T(8,128)} fusion(f32[2048,1024]{1,0:T(8,128)} %param.5, f32[256,8,8,128]{3,2,1,0:T(8,128)S(1)} %bitcast.20, f32[2048,256]{1,0:T(8,128)S(1)} %copy-done.2, s32[]{:T(128)S(6)} %select_n.46), kind=kOutput, calls=%fused_computation.3 | convolution fusion | flops 6445072384 | bytes 19922948 | tf_op jit(solution)/shard_map/dot_general | solution.py:64
  215.2 0.0 reduce-scatter.2.cloned.1.call-update
  215.2 0.0 copy-start.3
  215.2 0.0 all-reduce.5.cloned.1.call-start
  215.2 81.7 %reduce-scatter.2.cloned.1.call-done = f32[128,256]{1,0:T(8,128)} async-done(((f32[2048,256]{1,0:T(8,128)}), f32[128,256]{1,0:T(8,128)}) %reduce-scatter.2.cloned.1.call-update) | async-done | bytes 131088 | tf_op jit(solution)/shard_map/reduce_scatter | solution.py:63
  296.9 2.3 fusion.10
  299.3 0.0 all-reduce.5.cloned.1.call-update
  299.3 222.9 %all-reduce.5.cloned.1.call-done = f32[512,256]{1,0:T(8,128)} async-done(((f32[512,256]{1,0:T(8,128)}), f32[512,256]{1,0:T(8,128)}) %all-reduce.5.cloned.1.call-update) | async-done | bytes 524304 | tf_op jit(solution)/shard_map/psum | solution.py:75
  522.2 0.0 copy-start.1
  522.2 1.1 constant_dynamic-slice_fusion.1
  523.3 0.1 copy.11
  523.4 5.3 collective-permute-start
  528.7 0.1 copy.10
  528.8 1.0 collective-permute-done
  529.9 0.0 copy-done.3
  529.9 0.0 copy-done.1
  529.9 0.9 fusion.7
  (2 shorter events, 0.0 us)
Async XLA Ops:
  7.2 1.2 copy-start
  11.6 58.8 %all-to-all-start = ((f32[16,128,256]{2,1,0:T(8,128)}), f32[16,128,256]{2,1,0:T(8,128)S(1)}, u32[]{:S(2)}, u32[]{:S(2)}) async-start(f32[16,128,256]{2,1,0:T(8,128)} %stack.2), calls=%async_computation | async-start | bytes 4194304 | tf_op jit(solution)/shard_map/all_to_all | solution.py:49
  20.7 182.4 %all-reduce.3.cloned.1.call-start = ((), (), s32[]{:S(2)}) async-start(), calls=%async_computation.2 | async-start | bytes 4194304 | tf_op jit(solution)/shard_map/psum | solution.py:9
  72.0 0.7 copy-start.4
  72.0 224.9 %reduce-scatter.2.cloned.1.call-start = ((), (), s32[]{:S(2)}) async-start(), calls=%async_computation.3 | async-start | bytes 2228224 | tf_op jit(solution)/shard_map/reduce_scatter | solution.py:63
  203.0 1.6 copy-start.2
  215.2 314.7 %copy-start.3 = (f32[512,256]{1,0:T(8,128)S(1)}, f32[512,256]{1,0:T(8,128)}, u32[]{:S(2)}) copy-start(f32[512,256]{1,0:T(8,128)} %param.9) | copy-start | bytes 1572868
  215.2 307.0 %all-reduce.5.cloned.1.call-start = ((), (), s32[]{:S(2)}) async-start(), calls=%async_computation.4 | async-start | bytes 1048576 | tf_op jit(solution)/shard_map/psum | solution.py:75
  522.2 7.7 %copy-start.1 = (f32[512,256]{1,0:T(8,128)S(1)}, f32[512,256]{1,0:T(8,128)}, u32[]{:S(2)}) copy-start(f32[512,256]{1,0:T(8,128)} %all-reduce.5.cloned.1.call-done) | copy-start | bytes 1572868
  523.4 6.4 %collective-permute-start = (f32[256,256]{0,1:T(8,128)S(1)}, f32[256,256]{0,1:T(8,128)S(1)}, u32[]{:S(2)}, u32[]{:S(2)}) collective-permute-start(f32[256,256]{0,1:T(8,128)S(1)} %copy.11), channel_id=1, source_target_pairs={{0,1},{1,0},{2,3},{3,2},{4,5},{5,4},{6,7},{7,6},{8,9},{9,8},{10,11... | collective-permute-start | bytes 786440 | tf_op jit(solution)/shard_map/ppermute | solution.py:19
Sparse Core Ops, SparseCore 0:
  72.2 130.8 all-reduce.2
  215.3 81.5 reduce-scatter.1
  302.9 219.1 all-reduce.4
